TPU v7x, 32 devices: a whole 2x2x4 slice. The times are simulated.
32 devices in a mesh: section: 4 (over y, x), dp: 2 (over core), tensor: 4 (over z).
Axes of the slice: x: 2, y: 2, z: 4, core: 2. Of those that a mesh axis runs over, the one named last changes fastest.
Arguments:
- cotangent: bfloat16 [2, 256, 8192], P(None, 'dp', 'tensor'), may hold values from -6 to 6
- stash: bfloat16 [4, 2, 256, 8192], P('section', None, 'dp', 'tensor'), may hold values from -0.25 to 0.25
- factor_a: bfloat16 [4, 1024, 8192], P('section', 'dp', 'tensor'), may hold values from -0.0625 to 0.0625
- factor_b: bfloat16 [4, 8192, 1024], P('section', ('tensor', 'dp')), may hold values from -0.1875 to 0.1875
- block_vals: bfloat16 [4, 8, 128, 128], P('section', ('dp', 'tensor')), may hold values from -0.25 to 0.25
- block_rows: int32 [4, 8], P('section'), may hold values from 0 to 63, as said below
- block_cols: int32 [4, 8], P('section'), may hold values from 0 to 63, as said below
Outputs:
- grad_in: bfloat16 [4, 2, 256, 8192], P('section', None, 'dp', 'tensor')
- block_grad: float32 [4, 8, 128, 128], P('section', ('dp', 'tensor'))
Inputs may be any that keep to these rules, and one draw needn't show every extreme that they name: The support lies inside the diagonal part of each tensor shard. Within a section all (block_rows, block_cols) pairs are distinct. For every dp index o < 2, tensor index t < 4 and slot k < 1, the block at position (o * 4 + t) + k has both its row and its column block index in [t * 8192 // (128 * 4), (t + 1) * 8192 // (128 * 4)). `block_cols`: drawn together with block_rows; the same promise holds.
All inputs are finite; a program needn't handle non-finite values.
Results may differ from a plain program's by a relative error of at most 0.024.
Values may be sent and summed in bfloat16 or wider, within the bound.
A program may use at most 128 MiB of HBM per device.

v0:
```python
import jax
import jax.numpy as jnp
from jax import lax
from jax.sharding import PartitionSpec as P


def shifted(value, axis, steps):
    count = lax.axis_size(axis)
    initial, last = (max(0, -steps), min(count, count - steps))
    return lax.ppermute(value, axis, [(source, source + steps) for source in range(initial, last)])


def pass_back(grad_out):
    return shifted(grad_out, "section", -1)


def on_device(cotangent, stash, factor_a, factor_b, block_vals, block_rows, block_cols):
    sections = lax.axis_size("section")
    section_pos = lax.axis_index("section")
    tensor_pos = lax.axis_index("tensor")
    dp_count = lax.axis_size("dp")
    tensor_count = lax.axis_size("tensor")
    left_full, right_full, values = (
        lax.all_gather(factor_a[0], "dp", axis=0, tiled=True),
        lax.all_gather(factor_b[0], "dp", axis=0, tiled=True),
        lax.all_gather(block_vals[0], "dp", axis=0, tiled=True),
    )
    batches = stash.shape[1]
    tokens_here = stash.shape[2]
    local_width = stash.shape[3]
    block_size = block_vals.shape[-1]
    local_blocks = local_width // block_size

    def local_ids(table):
        grid = table[0].reshape(dp_count, tensor_count, -1)
        mine = lax.dynamic_index_in_dim(grid, tensor_pos, 1, keepdims=False)
        return mine.reshape(-1) - tensor_pos * local_blocks

    positions = jnp.arange(local_blocks, dtype=jnp.int32)[None, :]
    row_hits = local_ids(block_rows)[:, None] == positions
    col_hits = local_ids(block_cols)[:, None] == positions
    row_pick = row_hits.astype(jnp.bfloat16)
    row_double = jnp.concatenate([row_pick, row_pick], axis=0)
    col_pick = col_hits.astype(jnp.bfloat16)
    grad_sum = jnp.zeros((values.shape[0], block_size, block_size), jnp.float32)
    grads_in = jnp.zeros(stash.shape[1:], jnp.bfloat16)
    received = jnp.zeros((tokens_here, local_width), jnp.bfloat16)
    steps = batches + sections - 1
    for step_idx in range(steps):
        batch_pos = step_idx - (sections - 1 - section_pos)
        active = (batch_pos >= 0) & (batch_pos < batches)
        slot_pos = jnp.clip(batch_pos, 0, batches - 1)
        fresh = lax.dynamic_index_in_dim(cotangent, slot_pos, 0, keepdims=False)
        cot_now = jnp.where(section_pos == sections - 1, fresh, received)
        partial_value = jnp.einsum(
            "td,rd->tr", cot_now, left_full, preferred_element_type=jnp.float32
        )
        share = lax.psum_scatter(
            partial_value.astype(jnp.bfloat16), "tensor", scatter_dimension=1, tiled=True
        )
        rank_act = lax.all_gather(share, "tensor", axis=1, tiled=True)
        picked_cot = jnp.einsum(
            "tlc,nl->tnc",
            cot_now.reshape(tokens_here, local_blocks, block_size),
            col_pick,
            preferred_element_type=jnp.float32,
        ).astype(jnp.bfloat16)
        sparse_terms = jnp.einsum(
            "tnc,nrc->tnr", picked_cot, values, preferred_element_type=jnp.float32
        )
        upper_part = sparse_terms.astype(jnp.bfloat16)
        lower_part = (sparse_terms - upper_part.astype(jnp.float32)).astype(jnp.bfloat16)
        both_parts = jnp.concatenate([upper_part, lower_part], axis=1)
        sparse_grad = jnp.einsum(
            "tnr,nl->tlr", both_parts, row_double, preferred_element_type=jnp.float32
        )
        dense_grad = jnp.einsum(
            "tr,dr->td", rank_act, right_full, preferred_element_type=jnp.float32
        )
        grad_out = (dense_grad + sparse_grad.reshape(tokens_here, local_width)).astype(jnp.bfloat16)
        current = lax.dynamic_index_in_dim(grads_in, slot_pos, 0, keepdims=False)
        grads_in = lax.dynamic_update_index_in_dim(
            grads_in, jnp.where(active, grad_out, current), slot_pos, 0
        )
        stash_now = lax.dynamic_index_in_dim(stash[0], slot_pos, 0, keepdims=False)
        live_scale = active.astype(jnp.bfloat16)
        if step_idx + 1 < steps:
            received = pass_back(grad_out)
        picked_in = (
            jnp.einsum(
                "tlr,nl->tnr",
                stash_now.reshape(tokens_here, local_blocks, block_size),
                row_pick,
                preferred_element_type=jnp.float32,
            ).astype(jnp.bfloat16)
            * live_scale
        )
        grad_sum = grad_sum + jnp.einsum(
            "tnr,tnc->nrc", picked_in, picked_cot, preferred_element_type=jnp.float32
        )
    block_grad = lax.psum_scatter(
        grad_sum.astype(jnp.bfloat16), "dp", scatter_dimension=0, tiled=True
    ).astype(jnp.float32)
    return (grads_in[None], block_grad[None])


def solution(mesh):
    in_specs = (
        P(None, "dp", "tensor"),
        P("section", None, "dp", "tensor"),
        P("section", "dp", "tensor"),
        P("section", ("tensor", "dp"), None),
        P("section", ("dp", "tensor"), None, None),
        P("section", None),
        P("section", None),
    )
    out_specs = (P("section", None, "dp", "tensor"), P("section", ("dp", "tensor"), None, None))
    return jax.shard_map(
        on_device, mesh=mesh, in_specs=in_specs, out_specs=out_specs, check_vma=False
    )
```

profile of v0, /device:TPU:0, one launch (start us, length us, event | category | flops | bytes accessed | tf_op | source)
XLA Modules:
  0.0 300.2 jit_solution(10202126768568250833)
XLA Ops:
  8.0 17.9 %all-gather.6.cloned.1.call-done = bf16[1,1024,2048]{2,1,0:T(8,128)(2,1)} async-done(((bf16[1,512,2048]{2,1,0:T(8,128)(2,1)}), bf16[1,1024,2048]{2,1,0:T(8,128)(2,1)}) %all-gather.6.cloned.1.call-update) | async-done | bytes 4194320 | tf_op jit(solution)/shard_map/all_gather | solution.py:24
  25.9 4.6 %fusion.59 = bf16[128,1024]{1,0:T(8,128)(2,1)} fusion(bf16[1,1024,2048]{2,1,0:T(8,128)(2,1)} %all-gather.6.cloned.1.call-done, bf16[2,128,2048]{2,1,0:T(8,128)(2,1)} %param.7, s32[]{:T(128)S(6)} %min.16, pred[]{:T(512)S(6)} %eq.14), kind=kOutput, calls=%fused_computation.33 | convolution fusion | flops 537264128 | bytes 4980741 | tf_op jit(solution)/shard_map/td,rd->tr/dot_general | solution.py:55
  33.6 1.5 dynamic-slice_bitcast_fusion
  35.0 0.9 copy.71
  36.2 1.9 all-gather.2
  39.0 12.9 %reduce-scatter.7.cloned.1.call-done = bf16[128,256]{1,0:T(8,128)(2,1)} async-done(((bf16[128,1024]{1,0:T(8,128)(2,1)}), bf16[128,256]{1,0:T(8,128)(2,1)}) %reduce-scatter.7.cloned.1.call-update) | async-done | bytes 65552 | tf_op jit(solution)/shard_map/reduce_scatter | solution.py:58
  51.9 14.0 %all_gather.25 = bf16[128,1024]{1,0:T(8,128)(2,1)S(1)} all-gather(bf16[128,256]{1,0:T(8,128)(2,1)} %reduce-scatter.7.cloned.1.call-done), channel_id=1, replica_groups=mesh['section'=4,'dp'=2,'tensor'=4] {'tensor'}, dimensions={1}, use_global_device_ids=true | all-gather | bytes 327680 | tf_op jit(solution)/shard_map/all_gather | solution.py:61
  66.0 4.7 %bitcast_dynamic-update-slice_fusion.3 = (bf16[2,128,2048]{2,1,0:T(8,128)(2,1)S(1)}, bf16[128,2048]{1,0:T(8,128)(2,1)}) fusion(bf16[2,128,2048]{2,1,0:T(8,128)(2,1)S(1)} %broadcast_in_dim.36, s32[]{:T(128)S(6)} %min.16, pred[]{:T(512)S(6)} %and.17, f32[16,8,16,128]{3,2,1,0:T(8,128)S(1)} %bitcast.277, bf16[128,1024]{1,0:T(8,128)(2,1)S(1)} %all_gather.25, ...), kind=kOutput, calls=%fused_computation.83 | convolution fusion | flops 537657344 | bytes 6553605 | tf_op jit(solution)/shard_map/tr,dr->td/dot_general | solution.py:77
  70.7 1.3 collective-permute-start
  72.0 2.0 fusion.81
  74.0 1.1 copy.72
  75.1 2.0 copy.73
  77.1 0.9 fusion.83
  78.0 0.8 constant_dynamic-slice_fusion.2
  78.8 7.5 %collective-permute-done = bf16[128,2048]{1,0:T(8,128)(2,1)S(1)} collective-permute-done((bf16[128,2048]{1,0:T(8,128)(2,1)}, bf16[128,2048]{1,0:T(8,128)(2,1)S(1)}, u32[]{:S(2)}, u32[]{:S(2)}) %collective-permute-start) | collective-permute-done | bytes 524320 | tf_op jit(solution)/shard_map/ppermute | solution.py:10
  86.8 2.2 fusion.62
  89.8 20.7 %reduce-scatter.9.cloned.1.call-done = bf16[128,256]{1,0:T(8,128)(2,1)} async-done(((bf16[128,1024]{1,0:T(8,128)(2,1)}), bf16[128,256]{1,0:T(8,128)(2,1)}) %reduce-scatter.9.cloned.1.call-update) | async-done | bytes 65552 | tf_op jit(solution)/shard_map/reduce_scatter | solution.py:58
  110.4 14.2 %all_gather.28 = bf16[128,1024]{1,0:T(8,128)(2,1)S(1)} all-gather(bf16[128,256]{1,0:T(8,128)(2,1)} %reduce-scatter.9.cloned.1.call-done), channel_id=1, replica_groups=mesh['section'=4,'dp'=2,'tensor'=4] {'tensor'}, dimensions={1}, use_global_device_ids=true | all-gather | bytes 327680 | tf_op jit(solution)/shard_map/all_gather | solution.py:61
  124.6 4.8 %bitcast_dynamic-update-slice_fusion.2 = (bf16[2,128,2048]{2,1,0:T(8,128)(2,1)S(1)}, bf16[128,2048]{1,0:T(8,128)(2,1)}) fusion(bf16[2,128,2048]{2,1,0:T(8,128)(2,1)S(1)} %get-tuple-element.17, s32[]{:T(128)S(6)} %min.17, bf16[1,128,2048]{2,1,0:T(8,128)(2,1)} %constant_dynamic-slice_fusion.2, pred[]{:T(512)S(6)} %and.18, ...), kind=kOutput, calls=%fused_computation.80 | convolution fusion | flops 537657344 | bytes 7077893 | tf_op jit(solution)/shard_map/tr,dr->td/dot_general | solution.py:77
  129.4 1.3 collective-permute-start.1
  130.7 0.9 fusion.85
  131.6 1.1 copy.74
  132.8 0.9 fusion.87
  134.6 6.4 %collective-permute-done.1 = bf16[128,2048]{1,0:T(8,128)(2,1)S(1)} collective-permute-done((bf16[128,2048]{1,0:T(8,128)(2,1)}, bf16[128,2048]{1,0:T(8,128)(2,1)S(1)}, u32[]{:S(2)}, u32[]{:S(2)}) %collective-permute-start.1) | collective-permute-done | bytes 524320 | tf_op jit(solution)/shard_map/ppermute | solution.py:10
  141.4 2.2 fusion.65
  144.4 17.8 %reduce-scatter.11.cloned.1.call-done = bf16[128,256]{1,0:T(8,128)(2,1)} async-done(((bf16[128,1024]{1,0:T(8,128)(2,1)}), bf16[128,256]{1,0:T(8,128)(2,1)}) %reduce-scatter.11.cloned.1.call-update) | async-done | bytes 65552 | tf_op jit(solution)/shard_map/reduce_scatter | solution.py:58
  162.2 14.4 %all_gather.29 = bf16[128,1024]{1,0:T(8,128)(2,1)S(1)} all-gather(bf16[128,256]{1,0:T(8,128)(2,1)} %reduce-scatter.11.cloned.1.call-done), channel_id=1, replica_groups=mesh['section'=4,'dp'=2,'tensor'=4] {'tensor'}, dimensions={1}, use_global_device_ids=true | all-gather | bytes 327680 | tf_op jit(solution)/shard_map/all_gather | solution.py:61
  176.6 4.8 %bitcast_dynamic-update-slice_fusion.1 = (bf16[2,128,2048]{2,1,0:T(8,128)(2,1)S(1)}, bf16[128,2048]{1,0:T(8,128)(2,1)}) fusion(bf16[2,128,2048]{2,1,0:T(8,128)(2,1)S(1)} %get-tuple-element.19, s32[]{:T(128)S(6)} %min.18, bf16[1,128,2048]{2,1,0:T(8,128)(2,1)} %constant_dynamic-slice_fusion.1, pred[]{:T(512)S(6)} %and.19, ...), kind=kOutput, calls=%fused_computation.77 | convolution fusion | flops 537657344 | bytes 7077893 | tf_op jit(solution)/shard_map/tr,dr->td/dot_general | solution.py:77
  181.4 1.3 collective-permute-start.2
  182.7 0.9 fusion.116
  183.6 1.1 copy.75
  184.7 0.9 fusion.89
  185.6 0.9 constant_dynamic-slice_fusion
  186.6 6.2 %collective-permute-done.2 = bf16[128,2048]{1,0:T(8,128)(2,1)S(1)} collective-permute-done((bf16[128,2048]{1,0:T(8,128)(2,1)}, bf16[128,2048]{1,0:T(8,128)(2,1)S(1)}, u32[]{:S(2)}, u32[]{:S(2)}) %collective-permute-start.2) | collective-permute-done | bytes 524320 | tf_op jit(solution)/shard_map/ppermute | solution.py:10
  193.2 2.2 fusion.68
  196.2 17.9 %reduce-scatter.13.cloned.1.call-done = bf16[128,256]{1,0:T(8,128)(2,1)} async-done(((bf16[128,1024]{1,0:T(8,128)(2,1)}), bf16[128,256]{1,0:T(8,128)(2,1)}) %reduce-scatter.13.cloned.1.call-update) | async-done | bytes 65552 | tf_op jit(solution)/shard_map/reduce_scatter | solution.py:58
  214.0 14.2 %all_gather.30 = bf16[128,1024]{1,0:T(8,128)(2,1)S(1)} all-gather(bf16[128,256]{1,0:T(8,128)(2,1)} %reduce-scatter.13.cloned.1.call-done), channel_id=1, replica_groups=mesh['section'=4,'dp'=2,'tensor'=4] {'tensor'}, dimensions={1}, use_global_device_ids=true | all-gather | bytes 327680 | tf_op jit(solution)/shard_map/all_gather | solution.py:61
  228.2 4.0 %bitcast_dynamic-update-slice_fusion = (bf16[2,128,2048]{2,1,0:T(8,128)(2,1)S(1)}, bf16[128,2048]{1,0:T(8,128)(2,1)S(1)}) fusion(bf16[2,128,2048]{2,1,0:T(8,128)(2,1)S(1)} %get-tuple-element.21, s32[]{:T(128)S(6)} %min.19, bf16[1,128,2048]{2,1,0:T(8,128)(2,1)} %constant_dynamic-slice_fusion, pred[]{:T(512)S(6)} %and.20, ...), kind=kOutput, calls=%fused_computation.74 | convolution fusion | flops 537657344 | bytes 7077893 | tf_op jit(solution)/shard_map/tr,dr->td/dot_general | solution.py:77
  232.3 1.4 collective-permute-start.3
  234.4 1.0 copy.135
  235.3 8.4 %collective-permute-done.3 = bf16[128,2048]{1,0:T(8,128)(2,1)S(1)} collective-permute-done((bf16[128,2048]{1,0:T(8,128)(2,1)S(1)}, bf16[128,2048]{1,0:T(8,128)(2,1)S(1)}, u32[]{:S(2)}, u32[]{:S(2)}) %collective-permute-start.3) | collective-permute-done | bytes 524320 | tf_op jit(solution)/shard_map/ppermute | solution.py:10
  244.2 0.9 fusion.74
  245.1 4.4 %fusion.71 = bf16[128,1024]{1,0:T(8,128)(2,1)} fusion(bf16[1,1024,2048]{2,1,0:T(8,128)(2,1)} %all-gather.6.cloned.1.call-done, bf16[128,2048]{1,0:T(8,128)(2,1)S(1)} %collective-permute-done.3, bf16[2,128,2048]{2,1,0:T(8,128)(2,1)S(1)} %copy-done.3, s32[]{:T(128)S(6)} %min.20, pred[]{:T(512)S(6)} %eq.14), kind=kOutput, calls=%fused_computation.37 | convolution fusion | flops 537264128 | bytes 5505029 | tf_op jit(solution)/shard_map/td,rd->tr/dot_general | solution.py:55
  250.2 1.0 reduce-scatter.17.cloned.1.call-done
  251.2 1.4 bitcast_convert_fusion
  252.5 22.0 %reduce-scatter.15.cloned.1.call-done = bf16[128,256]{1,0:T(8,128)(2,1)} async-done(((bf16[128,1024]{1,0:T(8,128)(2,1)}), bf16[128,256]{1,0:T(8,128)(2,1)}) %reduce-scatter.15.cloned.1.call-update) | async-done | bytes 65552 | tf_op jit(solution)/shard_map/reduce_scatter | solution.py:58
  274.5 14.2 %all_gather.31 = bf16[128,1024]{1,0:T(8,128)(2,1)S(1)} all-gather(bf16[128,256]{1,0:T(8,128)(2,1)} %reduce-scatter.15.cloned.1.call-done), channel_id=1, replica_groups=mesh['section'=4,'dp'=2,'tensor'=4] {'tensor'}, dimensions={1}, use_global_device_ids=true | all-gather | bytes 327680 | tf_op jit(solution)/shard_map/all_gather | solution.py:61
  288.7 4.7 %fusion.56 = bf16[1,2,128,2048]{3,2,1,0:T(8,128)(2,1)} fusion(bf16[1,2,128,2048]{3,2,1,0:T(8,128)(2,1)} %copy.135, s32[]{:T(128)S(6)} %min.20, bf16[128,1024]{1,0:T(8,128)(2,1)S(1)} %all_gather.31, bf16[1,2048,1024]{2,1,0:T(8,128)(2,1)} %all-gather.8.cloned.1.call-done, f32[16,8,16,128]{3,2,1,0:T(8,128)S(1)} %bitcast.276, ...), kind=kOutput, calls=%fused_computation.32 | convolution fusion | flops 537657344 | bytes 6553605 | tf_op jit(solution)/shard_map/tr,dr->td/dot_general | solution.py:77
  (89 shorter events, 10.9 us)
Async XLA Ops:
  7.2 18.8 %all-gather.6.cloned.1.call-start = ((), (), s32[]{:S(2)}) async-start(), calls=%async_computation.12 | async-start | bytes 6291456 | tf_op jit(solution)/shard_map/all_gather | solution.py:24
  7.9 23.4 %copy-start.3 = (bf16[2,128,2048]{2,1,0:T(8,128)(2,1)S(1)}, bf16[2,128,2048]{2,1,0:T(8,128)(2,1)}, u32[]{:S(2)}) copy-start(bf16[2,128,2048]{2,1,0:T(8,128)(2,1)} %param.7) | copy-start | bytes 3145732
  7.9 44.0 %reduce-scatter.7.cloned.1.call-start = ((), (), s32[]{:S(2)}) async-start(), calls=%async_computation.6 | async-start | bytes 327680 | tf_op jit(solution)/shard_map/reduce_scatter | solution.py:58
  8.0 24.1 %copy-start.13 = (s32[1,8]{1,0:T(1,128)S(1)}, s32[1,8]{1,0:T(1,128)}, u32[]{:S(2)}) copy-start(s32[1,8]{1,0:T(1,128)} %param.12) | copy-start | bytes 100
  8.0 24.8 %copy-start.14 = (s32[1,8]{1,0:T(1,128)S(1)}, s32[1,8]{1,0:T(1,128)}, u32[]{:S(2)}) copy-start(s32[1,8]{1,0:T(1,128)} %param.13) | copy-start | bytes 100
  8.0 25.6 %copy-start.4 = (bf16[1,2,128,2048]{3,2,1,0:T(8,128)(2,1)S(1)}, bf16[1,2,128,2048]{3,2,1,0:T(8,128)(2,1)}, u32[]{:S(2)}) copy-start(bf16[1,2,128,2048]{3,2,1,0:T(8,128)(2,1)} %param.8) | copy-start | bytes 3145732
  30.5 35.3 %all-gather.8.cloned.1.call-start = ((), (), s32[]{:S(2)}) async-start(), calls=%async_computation.13 | async-start | bytes 6291456 | tf_op jit(solution)/shard_map/all_gather | solution.py:25
  31.3 79.2 %reduce-scatter.9.cloned.1.call-start = ((), (), s32[]{:S(2)}) async-start(), calls=%async_computation.7 | async-start | bytes 327680 | tf_op jit(solution)/shard_map/reduce_scatter | solution.py:58
  31.3 4.8 %copy-start.12 = (bf16[1,1,128,128]{3,2,1,0:T(8,128)(2,1)S(1)}, bf16[1,1,128,128]{3,2,1,0:T(8,128)(2,1)}, u32[]{:S(2)}) copy-start(bf16[1,1,128,128]{3,2,1,0:T(8,128)(2,1)} %param.11) | copy-start | bytes 98308
  70.7 15.7 %collective-permute-start = (bf16[128,2048]{1,0:T(8,128)(2,1)}, bf16[128,2048]{1,0:T(8,128)(2,1)S(1)}, u32[]{:S(2)}, u32[]{:S(2)}) collective-permute-start(bf16[128,2048]{1,0:T(8,128)(2,1)} %get-tuple-element.18), channel_id=1, source_target_pairs={{8,0},{16,8},{24,16},{9,1},{17,9},{25,17},{10,2},{18,10},{26,18},{... | collective-permute-start | bytes 1572872 | tf_op jit(solution)/shard_map/ppermute | solution.py:10
  77.1 9.7 %copy-start = (bf16[1,1024,2048]{2,1,0:T(8,128)(2,1)S(1)}, bf16[1,1024,2048]{2,1,0:T(8,128)(2,1)}, u32[]{:S(2)}) copy-start(bf16[1,1024,2048]{2,1,0:T(8,128)(2,1)} %all-gather.6.cloned.1.call-done) | copy-start | bytes 12582916
  89.1 73.1 %reduce-scatter.11.cloned.1.call-start = ((), (), s32[]{:S(2)}) async-start(), calls=%async_computation.8 | async-start | bytes 327680 | tf_op jit(solution)/shard_map/reduce_scatter | solution.py:58
  110.4 20.3 %copy-start.5 = (bf16[16,8,16,128]{3,2,1,0:T(8,128)(2,1)S(1)}, bf16[16,8,16,128]{3,2,1,0:T(8,128)(2,1)}, u32[]{:S(2)}) copy-start(bf16[16,8,16,128]{3,2,1,0:T(8,128)(2,1)} %copy.73) | copy-start | bytes 1572868
  129.4 11.6 %collective-permute-start.1 = (bf16[128,2048]{1,0:T(8,128)(2,1)}, bf16[128,2048]{1,0:T(8,128)(2,1)S(1)}, u32[]{:S(2)}, u32[]{:S(2)}) collective-permute-start(bf16[128,2048]{1,0:T(8,128)(2,1)} %get-tuple-element.20), channel_id=1, source_target_pairs={{8,0},{16,8},{24,16},{9,1},{17,9},{25,17},{10,2},{18,10},{26,18},{... | collective-permute-start | bytes 1572872 | tf_op jit(solution)/shard_map/ppermute | solution.py:10
  132.8 8.7 %copy-start.1 = (bf16[1,1024,2048]{2,1,0:T(8,128)(2,1)S(1)}, bf16[1,1024,2048]{2,1,0:T(8,128)(2,1)}, u32[]{:S(2)}) copy-start(bf16[1,1024,2048]{2,1,0:T(8,128)(2,1)} %all-gather.6.cloned.1.call-done) | copy-start | bytes 12582916
  143.7 70.3 %reduce-scatter.13.cloned.1.call-start = ((), (), s32[]{:S(2)}) async-start(), calls=%async_computation.9 | async-start | bytes 327680 | tf_op jit(solution)/shard_map/reduce_scatter | solution.py:58
  144.4 38.3 %copy-start.9 = (bf16[128,2,128]{2,1,0:T(2,128)(2,1)S(1)}, bf16[128,2,128]{2,1,0:T(2,128)(2,1)}, u32[]{:S(2)}) copy-start(bf16[128,2,128]{2,1,0:T(2,128)(2,1)} %fusion.81) | copy-start | bytes 196612
  181.4 11.4 %collective-permute-start.2 = (bf16[128,2048]{1,0:T(8,128)(2,1)}, bf16[128,2048]{1,0:T(8,128)(2,1)S(1)}, u32[]{:S(2)}, u32[]{:S(2)}) collective-permute-start(bf16[128,2048]{1,0:T(8,128)(2,1)} %get-tuple-element.22), channel_id=1, source_target_pairs={{8,0},{16,8},{24,16},{9,1},{17,9},{25,17},{10,2},{18,10},{26,18},{... | collective-permute-start | bytes 1572872 | tf_op jit(solution)/shard_map/ppermute | solution.py:10
  184.7 8.5 %copy-start.2 = (bf16[1,1024,2048]{2,1,0:T(8,128)(2,1)S(1)}, bf16[1,1024,2048]{2,1,0:T(8,128)(2,1)}, u32[]{:S(2)}) copy-start(bf16[1,1024,2048]{2,1,0:T(8,128)(2,1)} %all-gather.6.cloned.1.call-done) | copy-start | bytes 12582916
  195.5 55.6 %reduce-scatter.17.cloned.1.call-start = ((), (), s32[]{:S(2)}) async-start(), calls=%async_computation.11 | async-start | bytes 98304 | tf_op jit(solution)/shard_map/reduce_scatter | solution.py:101
  195.8 37.9 %copy-start.6 = (f32[2,128,128]{2,1,0:T(8,128)S(1)}, f32[2,128,128]{2,1,0:T(8,128)}, u32[]{:S(2)}) copy-start(f32[2,128,128]{2,1,0:T(8,128)} %fusion.116) | copy-start | bytes 393220
  214.0 19.7 %copy-start.8 = (bf16[128,2,128]{2,1,0:T(2,128)(2,1)S(1)}, bf16[128,2,128]{2,1,0:T(2,128)(2,1)}, u32[]{:S(2)}) copy-start(bf16[128,2,128]{2,1,0:T(2,128)(2,1)} %fusion.83) | copy-start | bytes 196612
  214.0 19.9 %copy-start.10 = (bf16[128,2,128]{2,1,0:T(2,128)(2,1)S(1)}, bf16[128,2,128]{2,1,0:T(2,128)(2,1)}, u32[]{:S(2)}) copy-start(bf16[128,2,128]{2,1,0:T(2,128)(2,1)} %fusion.85) | copy-start | bytes 196612
  214.0 20.1 %copy-start.11 = (bf16[128,2,128]{2,1,0:T(2,128)(2,1)S(1)}, bf16[128,2,128]{2,1,0:T(2,128)(2,1)}, u32[]{:S(2)}) copy-start(bf16[128,2,128]{2,1,0:T(2,128)(2,1)} %fusion.87) | copy-start | bytes 196612
  232.2 12.0 %copy-start.7 = (bf16[128,2,128]{2,1,0:T(2,128)(2,1)S(1)}, bf16[128,2,128]{2,1,0:T(2,128)(2,1)}, u32[]{:S(2)}) copy-start(bf16[128,2,128]{2,1,0:T(2,128)(2,1)} %fusion.89) | copy-start | bytes 196612
  232.3 11.5 %collective-permute-start.3 = (bf16[128,2048]{1,0:T(8,128)(2,1)S(1)}, bf16[128,2048]{1,0:T(8,128)(2,1)S(1)}, u32[]{:S(2)}, u32[]{:S(2)}) collective-permute-start(bf16[128,2048]{1,0:T(8,128)(2,1)S(1)} %get-tuple-element.24), channel_id=1, source_target_pairs={{8,0},{16,8},{24,16},{9,1},{17,9},{25,17},{10,2},{18,10},{26,18},{... | collective-permute-start | bytes 1572872 | tf_op jit(solution)/shard_map/ppermute | solution.py:10
  245.1 29.4 %reduce-scatter.15.cloned.1.call-start = ((), (), s32[]{:S(2)}) async-start(), calls=%async_computation.10 | async-start | bytes 327680 | tf_op jit(solution)/shard_map/reduce_scatter | solution.py:58
Sparse Core Ops, SparseCore 0:
  9.5 16.3 all-gather.5
  30.7 21.1 reduce-scatter.6
  53.4 11.8 all-gather.7
  89.2 21.1 reduce-scatter.8
  143.8 18.3 reduce-scatter.10
  195.6 18.3 reduce-scatter.12
  245.2 5.9 reduce-scatter.16
  253.4 21.0 reduce-scatter.14
where the time goes:
time: 301 us; the launch traced here: 300 us
  waiting for transfers between devices  140 us (47%)
  blocking collectives  72.7 us (24%)
  matrix products  51 us (17%)
  between operations  14.6 us (5%)
  local copies, waits for them, and re-layouts  12.8 us (4%)
  starting transfers between devices  5.59 us (2%)
  other arithmetic  3.35 us (1%)
    reduce_scatter x5, waiting for transfers between devices, on_device(): lax.psum_scatter(partial_value.astype(jnp.bfloat16), 'tensor', scatter_di...  91.2 us
    all_gather x5, blocking collectives, on_device(): rank_act = lax.all_gather(share, 'tensor', axis=1, tiled=True)  70.8 us
    ppermute x4, waiting for transfers between devices, shifted(): lax.ppermute(value, axis, [(source, source + steps) for source in range(i...  28.5 us
    dot_general x5, matrix products, on_device(): jnp.einsum('tr,dr->td', rank_act, right_full, preferred_element_type=jnp....  23.1 us
    all_gather x1, waiting for transfers between devices, on_device(): lax.all_gather(factor_a[0], 'dp', axis=0, tiled=True)  17.9 us
    dot_general x5, matrix products, on_device(): jnp.einsum('td,rd->tr', cot_now, left_full, preferred_element_type=jnp.fl...  15.7 us
    unnamed x43, local copies, waits for them, and re-layouts  9.95 us
  transfers between devices with their start and end apart: 12, of which 11 were waited for; matrix products, arithmetic and copies ran while one was open for 10% of the time, Pallas kernels for 0%

commit v1 on v0

--- a/solution.py
+++ b/solution.py
@@ -58,7 +58,6 @@
         share = lax.psum_scatter(
             partial_value.astype(jnp.bfloat16), "tensor", scatter_dimension=1, tiled=True
         )
-        rank_act = lax.all_gather(share, "tensor", axis=1, tiled=True)
         picked_cot = jnp.einsum(
             "tlc,nl->tnc",
             cot_now.reshape(tokens_here, local_blocks, block_size),
@@ -74,9 +73,51 @@
         sparse_grad = jnp.einsum(
             "tnr,nl->tlr", both_parts, row_double, preferred_element_type=jnp.float32
         )
+        z1 = lax.axis_size("tensor")
+        side_arr = lax.axis_index("tensor")
+        state_now, k_now, value_now = (z1, side_arr, share.shape[1])
+        cards = []
+        kk = 0
+        while kk < state_now:
+            cards.append((kk, (kk + 1) % state_now))
+            kk += 1
+        rack = []
+        kk = 0
+        while kk < state_now:
+            rack.append((kk, (kk - 1) % state_now))
+            kk += 1
+        current_value = state_now // 2
+        formed = outer = share
         dense_grad = jnp.einsum(
-            "tr,dr->td", rank_act, right_full, preferred_element_type=jnp.float32
+            "tr,dr->td",
+            share,
+            lax.dynamic_slice_in_dim(right_full, k_now * value_now, share.shape[1], axis=1),
+            preferred_element_type=jnp.float32,
         )
+        dev = 1
+        while dev < current_value + 1:
+            formed = lax.ppermute(formed, "tensor", cards)
+            if dev < state_now - current_value:
+                outer = lax.ppermute(outer, "tensor", rack)
+                far_arr = jnp.einsum(
+                    "tr,dr->td",
+                    outer,
+                    lax.dynamic_slice_in_dim(
+                        right_full, (k_now + dev) % state_now * value_now, outer.shape[1], axis=1
+                    ),
+                    preferred_element_type=jnp.float32,
+                )
+                dense_grad = dense_grad + far_arr
+            everything = jnp.einsum(
+                "tr,dr->td",
+                formed,
+                lax.dynamic_slice_in_dim(
+                    right_full, (k_now - dev) % state_now * value_now, formed.shape[1], axis=1
+                ),
+                preferred_element_type=jnp.float32,
+            )
+            dense_grad = dense_grad + everything
+            dev += 1
         grad_out = (dense_grad + sparse_grad.reshape(tokens_here, local_width)).astype(jnp.bfloat16)
         current = lax.dynamic_index_in_dim(grads_in, slot_pos, 0, keepdims=False)
         grads_in = lax.dynamic_update_index_in_dim(

time: 301 us -> 285 us (0.947)
  blocking collectives: 72.7 us -> 1.85 us
  waiting for transfers between devices: 140 us -> 181 us
  starting transfers between devices: 5.59 us -> 17.5 us
    all_gather x5 -> x0, blocking collectives: 70.8 us -> none  [on_device(): rank_act = lax.all_gather(share, 'tensor', axis=1, tiled=True)]
    ppermute x0 -> x15, waiting for transfers between devices: none -> 29.2 us  [the longest x10 29.2 us: on_device(): formed = lax.ppermute(formed, 'tensor', cards)]
    ppermute x0 -> x15, starting transfers between devices: none -> 11.9 us  [the longest x10 9.79 us: on_device(): formed = lax.ppermute(formed, 'tensor', cards)]
    all_gather x1, waiting for transfers between devices: 0.01 us -> 11.4 us  [on_device(): lax.all_gather(factor_b[0], 'dp', axis=0, tiled=True)]
    dot_general x5 -> x20, matrix products: 23.1 us -> 25.9 us  [the longest x5 8.82 us: on_device(): jnp.einsum('tr,dr->td', share, lax.dynamic_slice_in_dim(right_full, k_now...]
    unnamed x43 -> x63, local copies, waits for them, and re-layouts: 9.95 us -> 10.8 us
  transfers between devices with their start and end apart: 12 -> 27, of which waited for: 11 -> 21; matrix products, arithmetic and copies ran while one was open for 10% -> 17% of each run, Pallas kernels for 0% -> 0%
where the time goes in v1:
time: 285 us; the launch traced here: 284 us
  waiting for transfers between devices  181 us (64%)
  matrix products  52.1 us (18%)
  starting transfers between devices  17.5 us (6%)
  between operations  14.9 us (5%)
  local copies, waits for them, and re-layouts  13.7 us (5%)
  other arithmetic  3.35 us (1%)
    reduce_scatter x5, waiting for transfers between devices, on_device(): lax.psum_scatter(partial_value.astype(jnp.bfloat16), 'tensor', scatter_di...  89.6 us
    ppermute x4, waiting for transfers between devices, shifted(): lax.ppermute(value, axis, [(source, source + steps) for source in range(i...  30.3 us
    ppermute x10, waiting for transfers between devices, on_device(): formed = lax.ppermute(formed, 'tensor', cards)  29.2 us
    all_gather x1, waiting for transfers between devices, on_device(): lax.all_gather(factor_a[0], 'dp', axis=0, tiled=True)  17.9 us
    dot_general x5, matrix products, on_device(): jnp.einsum('td,rd->tr', cot_now, left_full, preferred_element_type=jnp.fl...  15.7 us
    all_gather x1, waiting for transfers between devices, on_device(): lax.all_gather(factor_b[0], 'dp', axis=0, tiled=True)  11.4 us
    unnamed x63, local copies, waits for them, and re-layouts  10.8 us
    ppermute x10, starting transfers between devices, on_device(): formed = lax.ppermute(formed, 'tensor', cards)  9.79 us
  transfers between devices with their start and end apart: 27, of which 21 were waited for; matrix products, arithmetic and copies ran while one was open for 17% of the time, Pallas kernels for 0%

profile of v1, /device:TPU:0, one launch (start us, length us, event | category | flops | bytes accessed | tf_op | source)
XLA Modules:
  0.0 284.5 jit_solution(15317015601307418098)
XLA Ops:
  8.0 17.9 %all-gather.6.cloned.1.call-done = bf16[1,1024,2048]{2,1,0:T(8,128)(2,1)} async-done(((bf16[1,512,2048]{2,1,0:T(8,128)(2,1)}), bf16[1,1024,2048]{2,1,0:T(8,128)(2,1)}) %all-gather.6.cloned.1.call-update) | async-done | bytes 4194320 | tf_op jit(solution)/shard_map/all_gather | solution.py:24
  25.9 4.6 %fusion.23 = bf16[128,1024]{1,0:T(8,128)(2,1)} fusion(bf16[1,1024,2048]{2,1,0:T(8,128)(2,1)} %all-gather.6.cloned.1.call-done, bf16[2,128,2048]{2,1,0:T(8,128)(2,1)} %param.7, s32[]{:T(128)S(6)} %min.16, pred[]{:T(512)S(6)} %eq.49), kind=kOutput, calls=%fused_computation.38 | convolution fusion | flops 537264128 | bytes 4980741 | tf_op jit(solution)/shard_map/td,rd->tr/dot_general | solution.py:55
  33.6 1.4 dynamic-slice_bitcast_fusion
  36.2 1.9 all-gather.2
  39.0 12.9 %reduce-scatter.7.cloned.1.call-done = bf16[128,256]{1,0:T(8,128)(2,1)} async-done(((bf16[128,1024]{1,0:T(8,128)(2,1)}), bf16[128,256]{1,0:T(8,128)(2,1)}) %reduce-scatter.7.cloned.1.call-update) | async-done | bytes 65552 | tf_op jit(solution)/shard_map/reduce_scatter | solution.py:58
  52.3 1.6 collective-permute-start.1
  53.9 11.4 %all-gather.8.cloned.1.call-done = bf16[1,2048,1024]{2,1,0:T(8,128)(2,1)} async-done(((bf16[1,1024,1024]{2,1,0:T(8,128)(2,1)}), bf16[1,2048,1024]{2,1,0:T(8,128)(2,1)}) %all-gather.8.cloned.1.call-update) | async-done | bytes 4194320 | tf_op jit(solution)/shard_map/all_gather | solution.py:25
  65.3 1.9 fusion.77
  67.2 1.8 collective-permute-start.2
  69.0 1.7 convolution_add_fusion.14
  71.3 2.2 collective-permute-done.2
  73.6 1.5 bitcast_dynamic-update-slice_fusion.3
  78.5 2.0 copy.73
  82.2 8.3 %collective-permute-done.3 = bf16[128,2048]{1,0:T(8,128)(2,1)S(1)} collective-permute-done((bf16[128,2048]{1,0:T(8,128)(2,1)}, bf16[128,2048]{1,0:T(8,128)(2,1)S(1)}, u32[]{:S(2)}, u32[]{:S(2)}) %collective-permute-start.3) | collective-permute-done | bytes 524320 | tf_op jit(solution)/shard_map/ppermute | solution.py:10
  91.0 2.2 fusion.26
  93.9 18.8 %reduce-scatter.9.cloned.1.call-done = bf16[128,256]{1,0:T(8,128)(2,1)} async-done(((bf16[128,1024]{1,0:T(8,128)(2,1)}), bf16[128,256]{1,0:T(8,128)(2,1)}) %reduce-scatter.9.cloned.1.call-update) | async-done | bytes 65552 | tf_op jit(solution)/shard_map/reduce_scatter | solution.py:58
  113.1 1.5 collective-permute-start.5
  114.7 1.7 fusion.75
  116.4 3.0 %collective-permute-done.5 = bf16[128,256]{1,0:T(8,128)(2,1)S(1)} collective-permute-done((bf16[128,256]{1,0:T(8,128)(2,1)}, bf16[128,256]{1,0:T(8,128)(2,1)S(1)}, u32[]{:S(2)}, u32[]{:S(2)}) %collective-permute-start.5) | collective-permute-done | bytes 65568 | tf_op jit(solution)/shard_map/ppermute | solution.py:99
  119.4 1.7 convolution_add_fusion.11
  121.6 3.8 %collective-permute-done.6 = bf16[128,256]{1,0:T(8,128)(2,1)S(1)} collective-permute-done((bf16[128,256]{1,0:T(8,128)(2,1)S(1)}, bf16[128,256]{1,0:T(8,128)(2,1)S(1)}, u32[]{:S(2)}, u32[]{:S(2)}) %collective-permute-start.6) | collective-permute-done | bytes 65568 | tf_op jit(solution)/shard_map/ppermute | solution.py:99
  125.5 1.5 bitcast_dynamic-update-slice_fusion.2
  132.2 6.4 %collective-permute-done.7 = bf16[128,2048]{1,0:T(8,128)(2,1)S(1)} collective-permute-done((bf16[128,2048]{1,0:T(8,128)(2,1)}, bf16[128,2048]{1,0:T(8,128)(2,1)S(1)}, u32[]{:S(2)}, u32[]{:S(2)}) %collective-permute-start.7) | collective-permute-done | bytes 524320 | tf_op jit(solution)/shard_map/ppermute | solution.py:10
  139.1 2.2 fusion.29
  142.0 17.9 %reduce-scatter.11.cloned.1.call-done = bf16[128,256]{1,0:T(8,128)(2,1)} async-done(((bf16[128,1024]{1,0:T(8,128)(2,1)}), bf16[128,256]{1,0:T(8,128)(2,1)}) %reduce-scatter.11.cloned.1.call-update) | async-done | bytes 65552 | tf_op jit(solution)/shard_map/reduce_scatter | solution.py:58
  160.4 1.6 collective-permute-start.9
  161.9 1.7 fusion.73
  163.7 3.0 %collective-permute-done.9 = bf16[128,256]{1,0:T(8,128)(2,1)S(1)} collective-permute-done((bf16[128,256]{1,0:T(8,128)(2,1)}, bf16[128,256]{1,0:T(8,128)(2,1)S(1)}, u32[]{:S(2)}, u32[]{:S(2)}) %collective-permute-start.9) | collective-permute-done | bytes 65568 | tf_op jit(solution)/shard_map/ppermute | solution.py:99
  166.7 1.7 convolution_add_fusion.8
  168.9 3.8 %collective-permute-done.10 = bf16[128,256]{1,0:T(8,128)(2,1)S(1)} collective-permute-done((bf16[128,256]{1,0:T(8,128)(2,1)S(1)}, bf16[128,256]{1,0:T(8,128)(2,1)S(1)}, u32[]{:S(2)}, u32[]{:S(2)}) %collective-permute-start.10) | collective-permute-done | bytes 65568 | tf_op jit(solution)/shard_map/ppermute | solution.py:99
  172.7 1.5 bitcast_dynamic-update-slice_fusion.1
  178.7 7.1 %collective-permute-done.11 = bf16[128,2048]{1,0:T(8,128)(2,1)S(1)} collective-permute-done((bf16[128,2048]{1,0:T(8,128)(2,1)}, bf16[128,2048]{1,0:T(8,128)(2,1)S(1)}, u32[]{:S(2)}, u32[]{:S(2)}) %collective-permute-start.11) | collective-permute-done | bytes 524320 | tf_op jit(solution)/shard_map/ppermute | solution.py:10
  186.3 2.2 fusion.32
  189.2 18.0 %reduce-scatter.13.cloned.1.call-done = bf16[128,256]{1,0:T(8,128)(2,1)} async-done(((bf16[128,1024]{1,0:T(8,128)(2,1)}), bf16[128,256]{1,0:T(8,128)(2,1)}) %reduce-scatter.13.cloned.1.call-update) | async-done | bytes 65552 | tf_op jit(solution)/shard_map/reduce_scatter | solution.py:58
  207.6 1.6 collective-permute-start.13
  209.2 1.7 fusion.71
  211.0 2.9 %collective-permute-done.13 = bf16[128,256]{1,0:T(8,128)(2,1)S(1)} collective-permute-done((bf16[128,256]{1,0:T(8,128)(2,1)}, bf16[128,256]{1,0:T(8,128)(2,1)S(1)}, u32[]{:S(2)}, u32[]{:S(2)}) %collective-permute-start.13) | collective-permute-done | bytes 65568 | tf_op jit(solution)/shard_map/ppermute | solution.py:99
  213.9 1.7 convolution_add_fusion.5
  216.2 3.8 %collective-permute-done.14 = bf16[128,256]{1,0:T(8,128)(2,1)S(1)} collective-permute-done((bf16[128,256]{1,0:T(8,128)(2,1)S(1)}, bf16[128,256]{1,0:T(8,128)(2,1)S(1)}, u32[]{:S(2)}, u32[]{:S(2)}) %collective-permute-start.14) | collective-permute-done | bytes 65568 | tf_op jit(solution)/shard_map/ppermute | solution.py:99
  220.7 1.4 collective-permute-start.15
  223.8 8.5 %collective-permute-done.15 = bf16[128,2048]{1,0:T(8,128)(2,1)S(1)} collective-permute-done((bf16[128,2048]{1,0:T(8,128)(2,1)S(1)}, bf16[128,2048]{1,0:T(8,128)(2,1)S(1)}, u32[]{:S(2)}, u32[]{:S(2)}) %collective-permute-start.15) | collective-permute-done | bytes 524320 | tf_op jit(solution)/shard_map/ppermute | solution.py:10
  233.7 4.4 %fusion.35 = bf16[128,1024]{1,0:T(8,128)(2,1)} fusion(bf16[1,1024,2048]{2,1,0:T(8,128)(2,1)} %all-gather.6.cloned.1.call-done, bf16[128,2048]{1,0:T(8,128)(2,1)S(1)} %collective-permute-done.15, bf16[2,128,2048]{2,1,0:T(8,128)(2,1)S(1)} %copy-done.8, s32[]{:T(128)S(6)} %min.20, pred[]{:T(512)S(6)} %eq.49), kind=kOutput, calls=%fused_computation.42 | convolution fusion | flops 537264128 | bytes 5505029 | tf_op jit(solution)/shard_map/td,rd->tr/dot_general | solution.py:55
  241.2 22.0 %reduce-scatter.15.cloned.1.call-done = bf16[128,256]{1,0:T(8,128)(2,1)} async-done(((bf16[128,1024]{1,0:T(8,128)(2,1)}), bf16[128,256]{1,0:T(8,128)(2,1)}) %reduce-scatter.15.cloned.1.call-update) | async-done | bytes 65552 | tf_op jit(solution)/shard_map/reduce_scatter | solution.py:58
  263.6 1.6 collective-permute-start.17
  265.2 1.7 fusion.69
  267.0 2.9 %collective-permute-done.17 = bf16[128,256]{1,0:T(8,128)(2,1)S(1)} collective-permute-done((bf16[128,256]{1,0:T(8,128)(2,1)}, bf16[128,256]{1,0:T(8,128)(2,1)S(1)}, u32[]{:S(2)}, u32[]{:S(2)}) %collective-permute-start.17) | collective-permute-done | bytes 65568 | tf_op jit(solution)/shard_map/ppermute | solution.py:99
  269.9 1.7 convolution_add_fusion.2
  272.1 3.8 %collective-permute-done.18 = bf16[128,256]{1,0:T(8,128)(2,1)S(1)} collective-permute-done((bf16[128,256]{1,0:T(8,128)(2,1)S(1)}, bf16[128,256]{1,0:T(8,128)(2,1)S(1)}, u32[]{:S(2)}, u32[]{:S(2)}) %collective-permute-start.18) | collective-permute-done | bytes 65568 | tf_op jit(solution)/shard_map/ppermute | solution.py:99
  (149 shorter events, 37.0 us)
Async XLA Ops:
  7.2 18.8 %all-gather.6.cloned.1.call-start = ((), (), s32[]{:S(2)}) async-start(), calls=%async_computation.12 | async-start | bytes 6291456 | tf_op jit(solution)/shard_map/all_gather | solution.py:24
  7.9 23.5 %copy-start.8 = (bf16[2,128,2048]{2,1,0:T(8,128)(2,1)S(1)}, bf16[2,128,2048]{2,1,0:T(8,128)(2,1)}, u32[]{:S(2)}) copy-start(bf16[2,128,2048]{2,1,0:T(8,128)(2,1)} %param.7) | copy-start | bytes 3145732
  7.9 44.0 %reduce-scatter.7.cloned.1.call-start = ((), (), s32[]{:S(2)}) async-start(), calls=%async_computation.6 | async-start | bytes 327680 | tf_op jit(solution)/shard_map/reduce_scatter | solution.py:58
  8.0 24.1 %copy-start.23 = (s32[1,8]{1,0:T(1,128)S(1)}, s32[1,8]{1,0:T(1,128)}, u32[]{:S(2)}) copy-start(s32[1,8]{1,0:T(1,128)} %param.12) | copy-start | bytes 100
  8.0 24.9 %copy-start.24 = (s32[1,8]{1,0:T(1,128)S(1)}, s32[1,8]{1,0:T(1,128)}, u32[]{:S(2)}) copy-start(s32[1,8]{1,0:T(1,128)} %param.13) | copy-start | bytes 100
  8.0 25.6 %copy-start.9 = (bf16[1,2,128,2048]{3,2,1,0:T(8,128)(2,1)S(1)}, bf16[1,2,128,2048]{3,2,1,0:T(8,128)(2,1)}, u32[]{:S(2)}) copy-start(bf16[1,2,128,2048]{3,2,1,0:T(8,128)(2,1)} %param.8) | copy-start | bytes 3145732
  30.5 34.8 %all-gather.8.cloned.1.call-start = ((), (), s32[]{:S(2)}) async-start(), calls=%async_computation.13 | async-start | bytes 6291456 | tf_op jit(solution)/shard_map/all_gather | solution.py:25
  31.3 81.4 %reduce-scatter.9.cloned.1.call-start = ((), (), s32[]{:S(2)}) async-start(), calls=%async_computation.7 | async-start | bytes 327680 | tf_op jit(solution)/shard_map/reduce_scatter | solution.py:58
  51.9 17.2 %collective-permute-start = (bf16[128,256]{1,0:T(8,128)(2,1)}, bf16[128,256]{1,0:T(8,128)(2,1)S(1)}, u32[]{:S(2)}, u32[]{:S(2)}) collective-permute-start(bf16[128,256]{1,0:T(8,128)(2,1)} %reduce-scatter.7.cloned.1.call-done), channel_id=1, source_target_pairs={{0,3},{1,0},{2,1},{3,2},{4,7},{5,4},{6,5},{7,6},{8,11},{9,8},{10,9... | collective-permute-start | bytes 196616 | tf_op jit(solution)/shard_map/ppermute | solution.py:101
  52.3 14.9 %collective-permute-start.1 = (bf16[128,256]{1,0:T(8,128)(2,1)}, bf16[128,256]{1,0:T(8,128)(2,1)S(1)}, u32[]{:S(2)}, u32[]{:S(2)}) collective-permute-start(bf16[128,256]{1,0:T(8,128)(2,1)} %reduce-scatter.7.cloned.1.call-done), channel_id=1, source_target_pairs={{0,1},{1,2},{2,3},{3,0},{4,5},{5,6},{6,7},{7,4},{8,9},{9,10},{10,1... | collective-permute-start | bytes 196616 | tf_op jit(solution)/shard_map/ppermute | solution.py:99
  67.2 6.2 %collective-permute-start.2 = (bf16[128,256]{1,0:T(8,128)(2,1)S(1)}, bf16[128,256]{1,0:T(8,128)(2,1)S(1)}, u32[]{:S(2)}, u32[]{:S(2)}) collective-permute-start(bf16[128,256]{1,0:T(8,128)(2,1)S(1)} %collective-permute-done.1), channel_id=1, source_target_pairs={{0,1},{1,2},{2,3},{3,0},{4,5},{5,6},{6,7},{7,4},{8,9},{9,10},{10,1... | collective-permute-start | bytes 196616 | tf_op jit(solution)/shard_map/ppermute | solution.py:99
  75.1 15.4 %collective-permute-start.3 = (bf16[128,2048]{1,0:T(8,128)(2,1)}, bf16[128,2048]{1,0:T(8,128)(2,1)S(1)}, u32[]{:S(2)}, u32[]{:S(2)}) collective-permute-start(bf16[128,2048]{1,0:T(8,128)(2,1)} %get-tuple-element.18), channel_id=1, source_target_pairs={{8,0},{16,8},{24,16},{9,1},{17,9},{25,17},{10,2},{18,10},{26,18},{... | collective-permute-start | bytes 1572872 | tf_op jit(solution)/shard_map/ppermute | solution.py:10
  80.4 10.5 %copy-start.5 = (bf16[1,1024,2048]{2,1,0:T(8,128)(2,1)S(1)}, bf16[1,1024,2048]{2,1,0:T(8,128)(2,1)}, u32[]{:S(2)}) copy-start(bf16[1,1024,2048]{2,1,0:T(8,128)(2,1)} %all-gather.6.cloned.1.call-done) | copy-start | bytes 12582916
  93.2 66.7 %reduce-scatter.11.cloned.1.call-start = ((), (), s32[]{:S(2)}) async-start(), calls=%async_computation.8 | async-start | bytes 327680 | tf_op jit(solution)/shard_map/reduce_scatter | solution.py:58
  112.7 8.5 %copy-start.1 = (bf16[1,2048,1024]{2,1,0:T(8,128)(2,1)S(1)}, bf16[1,2048,1024]{2,1,0:T(8,128)(2,1)}, u32[]{:S(2)}) copy-start(bf16[1,2048,1024]{2,1,0:T(8,128)(2,1)} %all-gather.8.cloned.1.call-done) | copy-start | bytes 12582916
  112.7 12.8 %copy-start.12 = (bf16[1,128,2048]{2,1,0:T(8,128)(2,1)S(1)}, bf16[1,128,2048]{2,1,0:T(8,128)(2,1)}, u32[]{:S(2)}) copy-start(bf16[1,128,2048]{2,1,0:T(8,128)(2,1)} %constant_dynamic-slice_fusion.2) | copy-start | bytes 1572868
  112.7 6.8 %collective-permute-start.4 = (bf16[128,256]{1,0:T(8,128)(2,1)}, bf16[128,256]{1,0:T(8,128)(2,1)S(1)}, u32[]{:S(2)}, u32[]{:S(2)}) collective-permute-start(bf16[128,256]{1,0:T(8,128)(2,1)} %reduce-scatter.9.cloned.1.call-done), channel_id=1, source_target_pairs={{0,3},{1,0},{2,1},{3,2},{4,7},{5,4},{6,5},{7,6},{8,11},{9,8},{10,9... | collective-permute-start | bytes 196616 | tf_op jit(solution)/shard_map/ppermute | solution.py:101
  113.1 6.3 %collective-permute-start.5 = (bf16[128,256]{1,0:T(8,128)(2,1)}, bf16[128,256]{1,0:T(8,128)(2,1)S(1)}, u32[]{:S(2)}, u32[]{:S(2)}) collective-permute-start(bf16[128,256]{1,0:T(8,128)(2,1)} %reduce-scatter.9.cloned.1.call-done), channel_id=1, source_target_pairs={{0,1},{1,2},{2,3},{3,0},{4,5},{5,6},{6,7},{7,4},{8,9},{9,10},{10,1... | collective-permute-start | bytes 196616 | tf_op jit(solution)/shard_map/ppermute | solution.py:99
  119.4 6.1 %collective-permute-start.6 = (bf16[128,256]{1,0:T(8,128)(2,1)S(1)}, bf16[128,256]{1,0:T(8,128)(2,1)S(1)}, u32[]{:S(2)}, u32[]{:S(2)}) collective-permute-start(bf16[128,256]{1,0:T(8,128)(2,1)S(1)} %collective-permute-done.5), channel_id=1, source_target_pairs={{0,1},{1,2},{2,3},{3,0},{4,5},{5,6},{6,7},{7,4},{8,9},{9,10},{10,1... | collective-permute-start | bytes 196616 | tf_op jit(solution)/shard_map/ppermute | solution.py:99
  121.1 7.2 %copy-start.11 = (bf16[16,8,16,128]{3,2,1,0:T(8,128)(2,1)S(1)}, bf16[16,8,16,128]{3,2,1,0:T(8,128)(2,1)}, u32[]{:S(2)}) copy-start(bf16[16,8,16,128]{3,2,1,0:T(8,128)(2,1)} %copy.73) | copy-start | bytes 1572868
  127.0 11.6 %collective-permute-start.7 = (bf16[128,2048]{1,0:T(8,128)(2,1)}, bf16[128,2048]{1,0:T(8,128)(2,1)S(1)}, u32[]{:S(2)}, u32[]{:S(2)}) collective-permute-start(bf16[128,2048]{1,0:T(8,128)(2,1)} %get-tuple-element.20), channel_id=1, source_target_pairs={{8,0},{16,8},{24,16},{9,1},{17,9},{25,17},{10,2},{18,10},{26,18},{... | collective-permute-start | bytes 1572872 | tf_op jit(solution)/shard_map/ppermute | solution.py:10
  130.4 8.7 %copy-start.6 = (bf16[1,1024,2048]{2,1,0:T(8,128)(2,1)S(1)}, bf16[1,1024,2048]{2,1,0:T(8,128)(2,1)}, u32[]{:S(2)}) copy-start(bf16[1,1024,2048]{2,1,0:T(8,128)(2,1)} %all-gather.6.cloned.1.call-done) | copy-start | bytes 12582916
  141.3 65.9 %reduce-scatter.13.cloned.1.call-start = ((), (), s32[]{:S(2)}) async-start(), calls=%async_computation.9 | async-start | bytes 327680 | tf_op jit(solution)/shard_map/reduce_scatter | solution.py:58
  159.9 8.5 %copy-start.2 = (bf16[1,2048,1024]{2,1,0:T(8,128)(2,1)S(1)}, bf16[1,2048,1024]{2,1,0:T(8,128)(2,1)}, u32[]{:S(2)}) copy-start(bf16[1,2048,1024]{2,1,0:T(8,128)(2,1)} %all-gather.8.cloned.1.call-done) | copy-start | bytes 12582916
  159.9 12.8 %copy-start.13 = (bf16[1,128,2048]{2,1,0:T(8,128)(2,1)S(1)}, bf16[1,128,2048]{2,1,0:T(8,128)(2,1)}, u32[]{:S(2)}) copy-start(bf16[1,128,2048]{2,1,0:T(8,128)(2,1)} %constant_dynamic-slice_fusion.1) | copy-start | bytes 1572868
  159.9 6.8 %collective-permute-start.8 = (bf16[128,256]{1,0:T(8,128)(2,1)}, bf16[128,256]{1,0:T(8,128)(2,1)S(1)}, u32[]{:S(2)}, u32[]{:S(2)}) collective-permute-start(bf16[128,256]{1,0:T(8,128)(2,1)} %reduce-scatter.11.cloned.1.call-done), channel_id=1, source_target_pairs={{0,3},{1,0},{2,1},{3,2},{4,7},{5,4},{6,5},{7,6},{8,11},{9,8},{10,9... | collective-permute-start | bytes 196616 | tf_op jit(solution)/shard_map/ppermute | solution.py:101
  160.4 6.3 %collective-permute-start.9 = (bf16[128,256]{1,0:T(8,128)(2,1)}, bf16[128,256]{1,0:T(8,128)(2,1)S(1)}, u32[]{:S(2)}, u32[]{:S(2)}) collective-permute-start(bf16[128,256]{1,0:T(8,128)(2,1)} %reduce-scatter.11.cloned.1.call-done), channel_id=1, source_target_pairs={{0,1},{1,2},{2,3},{3,0},{4,5},{5,6},{6,7},{7,4},{8,9},{9,10},{10,1... | collective-permute-start | bytes 196616 | tf_op jit(solution)/shard_map/ppermute | solution.py:99
  166.7 6.1 %collective-permute-start.10 = (bf16[128,256]{1,0:T(8,128)(2,1)S(1)}, bf16[128,256]{1,0:T(8,128)(2,1)S(1)}, u32[]{:S(2)}, u32[]{:S(2)}) collective-permute-start(bf16[128,256]{1,0:T(8,128)(2,1)S(1)} %collective-permute-done.9), channel_id=1, source_target_pairs={{0,1},{1,2},{2,3},{3,0},{4,5},{5,6},{6,7},{7,4},{8,9},{9,10},{10,1... | collective-permute-start | bytes 196616 | tf_op jit(solution)/shard_map/ppermute | solution.py:99
  168.4 7.2 %copy-start.19 = (bf16[128,2,128]{2,1,0:T(2,128)(2,1)S(1)}, bf16[128,2,128]{2,1,0:T(2,128)(2,1)}, u32[]{:S(2)}) copy-start(bf16[128,2,128]{2,1,0:T(2,128)(2,1)} %fusion.45) | copy-start | bytes 196612
  174.3 11.6 %collective-permute-start.11 = (bf16[128,2048]{1,0:T(8,128)(2,1)}, bf16[128,2048]{1,0:T(8,128)(2,1)S(1)}, u32[]{:S(2)}, u32[]{:S(2)}) collective-permute-start(bf16[128,2048]{1,0:T(8,128)(2,1)} %get-tuple-element.22), channel_id=1, source_target_pairs={{8,0},{16,8},{24,16},{9,1},{17,9},{25,17},{10,2},{18,10},{26,18},{... | collective-permute-start | bytes 1572872 | tf_op jit(solution)/shard_map/ppermute | solution.py:10
  176.9 9.4 %copy-start.7 = (bf16[1,1024,2048]{2,1,0:T(8,128)(2,1)S(1)}, bf16[1,1024,2048]{2,1,0:T(8,128)(2,1)}, u32[]{:S(2)}) copy-start(bf16[1,1024,2048]{2,1,0:T(8,128)(2,1)} %all-gather.6.cloned.1.call-done) | copy-start | bytes 12582916
  188.6 51.2 %reduce-scatter.17.cloned.1.call-start = ((), (), s32[]{:S(2)}) async-start(), calls=%async_computation.11 | async-start | bytes 98304 | tf_op jit(solution)/shard_map/reduce_scatter | solution.py:142
  207.2 8.4 %copy-start.3 = (bf16[1,2048,1024]{2,1,0:T(8,128)(2,1)S(1)}, bf16[1,2048,1024]{2,1,0:T(8,128)(2,1)}, u32[]{:S(2)}) copy-start(bf16[1,2048,1024]{2,1,0:T(8,128)(2,1)} %all-gather.8.cloned.1.call-done) | copy-start | bytes 12582916
  207.2 12.8 %copy-start.14 = (bf16[1,128,2048]{2,1,0:T(8,128)(2,1)S(1)}, bf16[1,128,2048]{2,1,0:T(8,128)(2,1)}, u32[]{:S(2)}) copy-start(bf16[1,128,2048]{2,1,0:T(8,128)(2,1)} %constant_dynamic-slice_fusion) | copy-start | bytes 1572868
  207.2 6.7 %collective-permute-start.12 = (bf16[128,256]{1,0:T(8,128)(2,1)}, bf16[128,256]{1,0:T(8,128)(2,1)S(1)}, u32[]{:S(2)}, u32[]{:S(2)}) collective-permute-start(bf16[128,256]{1,0:T(8,128)(2,1)} %reduce-scatter.13.cloned.1.call-done), channel_id=1, source_target_pairs={{0,3},{1,0},{2,1},{3,2},{4,7},{5,4},{6,5},{7,6},{8,11},{9,8},{10,9... | collective-permute-start | bytes 196616 | tf_op jit(solution)/shard_map/ppermute | solution.py:101
  207.6 6.3 %collective-permute-start.13 = (bf16[128,256]{1,0:T(8,128)(2,1)}, bf16[128,256]{1,0:T(8,128)(2,1)S(1)}, u32[]{:S(2)}, u32[]{:S(2)}) collective-permute-start(bf16[128,256]{1,0:T(8,128)(2,1)} %reduce-scatter.13.cloned.1.call-done), channel_id=1, source_target_pairs={{0,1},{1,2},{2,3},{3,0},{4,5},{5,6},{6,7},{7,4},{8,9},{9,10},{10,1... | collective-permute-start | bytes 196616 | tf_op jit(solution)/shard_map/ppermute | solution.py:99
  213.9 6.1 %collective-permute-start.14 = (bf16[128,256]{1,0:T(8,128)(2,1)S(1)}, bf16[128,256]{1,0:T(8,128)(2,1)S(1)}, u32[]{:S(2)}, u32[]{:S(2)}) collective-permute-start(bf16[128,256]{1,0:T(8,128)(2,1)S(1)} %collective-permute-done.13), channel_id=1, source_target_pairs={{0,1},{1,2},{2,3},{3,0},{4,5},{5,6},{6,7},{7,4},{8,9},{9,10},{10,1... | collective-permute-start | bytes 196616 | tf_op jit(solution)/shard_map/ppermute | solution.py:99
  215.6 6.5 %copy-start.18 = (bf16[128,2,128]{2,1,0:T(2,128)(2,1)S(1)}, bf16[128,2,128]{2,1,0:T(2,128)(2,1)}, u32[]{:S(2)}) copy-start(bf16[128,2,128]{2,1,0:T(2,128)(2,1)} %fusion.47) | copy-start | bytes 196612
  215.6 6.8 %copy-start.20 = (bf16[128,2,128]{2,1,0:T(2,128)(2,1)S(1)}, bf16[128,2,128]{2,1,0:T(2,128)(2,1)}, u32[]{:S(2)}) copy-start(bf16[128,2,128]{2,1,0:T(2,128)(2,1)} %fusion.49) | copy-start | bytes 196612
  215.6 7.0 %copy-start.21 = (bf16[128,2,128]{2,1,0:T(2,128)(2,1)S(1)}, bf16[128,2,128]{2,1,0:T(2,128)(2,1)}, u32[]{:S(2)}) copy-start(bf16[128,2,128]{2,1,0:T(2,128)(2,1)} %fusion.51) | copy-start | bytes 196612
  220.7 12.1 %copy-start.17 = (bf16[128,2,128]{2,1,0:T(2,128)(2,1)S(1)}, bf16[128,2,128]{2,1,0:T(2,128)(2,1)}, u32[]{:S(2)}) copy-start(bf16[128,2,128]{2,1,0:T(2,128)(2,1)} %fusion.53) | copy-start | bytes 196612
  220.7 11.6 %collective-permute-start.15 = (bf16[128,2048]{1,0:T(8,128)(2,1)S(1)}, bf16[128,2048]{1,0:T(8,128)(2,1)S(1)}, u32[]{:S(2)}, u32[]{:S(2)}) collective-permute-start(bf16[128,2048]{1,0:T(8,128)(2,1)S(1)} %get-tuple-element.24), channel_id=1, source_target_pairs={{8,0},{16,8},{24,16},{9,1},{17,9},{25,17},{10,2},{18,10},{26,18},{... | collective-permute-start | bytes 1572872 | tf_op jit(solution)/shard_map/ppermute | solution.py:10
  233.6 29.5 %reduce-scatter.15.cloned.1.call-start = ((), (), s32[]{:S(2)}) async-start(), calls=%async_computation.10 | async-start | bytes 327680 | tf_op jit(solution)/shard_map/reduce_scatter | solution.py:58
  241.2 34.7 %copy-start.15 = (bf16[1,2,128,2048]{3,2,1,0:T(8,128)(2,1)S(1)}, bf16[1,2,128,2048]{3,2,1,0:T(8,128)(2,1)}, u32[]{:S(2)}) copy-start(bf16[1,2,128,2048]{3,2,1,0:T(8,128)(2,1)} %copy.135) | copy-start | bytes 3145732
  263.2 8.4 %copy-start.4 = (bf16[1,2048,1024]{2,1,0:T(8,128)(2,1)S(1)}, bf16[1,2048,1024]{2,1,0:T(8,128)(2,1)}, u32[]{:S(2)}) copy-start(bf16[1,2048,1024]{2,1,0:T(8,128)(2,1)} %all-gather.8.cloned.1.call-done) | copy-start | bytes 12582916
  263.2 6.7 %collective-permute-start.16 = (bf16[128,256]{1,0:T(8,128)(2,1)}, bf16[128,256]{1,0:T(8,128)(2,1)S(1)}, u32[]{:S(2)}, u32[]{:S(2)}) collective-permute-start(bf16[128,256]{1,0:T(8,128)(2,1)} %reduce-scatter.15.cloned.1.call-done), channel_id=1, source_target_pairs={{0,3},{1,0},{2,1},{3,2},{4,7},{5,4},{6,5},{7,6},{8,11},{9,8},{10,9... | collective-permute-start | bytes 196616 | tf_op jit(solution)/shard_map/ppermute | solution.py:101
  263.6 6.3 %collective-permute-start.17 = (bf16[128,256]{1,0:T(8,128)(2,1)}, bf16[128,256]{1,0:T(8,128)(2,1)S(1)}, u32[]{:S(2)}, u32[]{:S(2)}) collective-permute-start(bf16[128,256]{1,0:T(8,128)(2,1)} %reduce-scatter.15.cloned.1.call-done), channel_id=1, source_target_pairs={{0,1},{1,2},{2,3},{3,0},{4,5},{5,6},{6,7},{7,4},{8,9},{9,10},{10,1... | collective-permute-start | bytes 196616 | tf_op jit(solution)/shard_map/ppermute | solution.py:99
  269.9 6.1 %collective-permute-start.18 = (bf16[128,256]{1,0:T(8,128)(2,1)S(1)}, bf16[128,256]{1,0:T(8,128)(2,1)S(1)}, u32[]{:S(2)}, u32[]{:S(2)}) collective-permute-start(bf16[128,256]{1,0:T(8,128)(2,1)S(1)} %collective-permute-done.17), channel_id=1, source_target_pairs={{0,1},{1,2},{2,3},{3,0},{4,5},{5,6},{6,7},{7,4},{8,9},{9,10},{10,1... | collective-permute-start | bytes 196616 | tf_op jit(solution)/shard_map/ppermute | solution.py:99
  (4 other events, 16.7 us)
Sparse Core Ops, SparseCore 0:
  9.5 16.3 all-gather.5
  30.7 21.1 reduce-scatter.6
  53.4 11.8 all-gather.7
  93.4 19.2 reduce-scatter.8
  141.5 18.4 reduce-scatter.10
  188.7 18.4 reduce-scatter.12
  233.8 5.9 reduce-scatter.16
  242.1 21.0 reduce-scatter.14
